TPU v7x, 32 devices: a whole 2x2x4 slice. The times are simulated.
32 devices in a mesh: tilt: 2 (over y), dom: 16 (over z, x, core).
Axes of the slice: x: 2, y: 2, z: 4, core: 2. Of those that a mesh axis runs over, the one named last changes fastest.
Arguments:
- sections: bfloat16 [32, 256, 256], P('dom'), may hold values from -6 to 6
- images: bfloat16 [32, 4, 256, 256], P('dom', 'tilt'), may hold values from -6 to 6
- slice_rows: bfloat16 [4, 256, 256], P('tilt'), may hold values from -0.375 to 0.375
- slice_cols: bfloat16 [4, 256, 256], P('tilt'), may hold values from -0.375 to 0.375
- ctf_filter: bfloat16 [4, 256, 256], P('tilt'), may hold values from -0.375 to 0.375
- nbr_owner: int32 [32, 2, 8], P('dom'), may hold values from 0 to 15, all different within a row; in each aligned block of 4 rows (0 to 3, 4 to 7, ..., all dimensions but the last counted through in order) at most 4 rows name the same one
- nbr_local: int32 [32, 16], P('dom'), may hold values from 0 to 1
- nbr_side: int32 [32, 16], P('dom'), may hold values from 0 to 1
- nbr_weight: float32 [32, 16], P('dom'), may hold values from 0.25 to 2
Outputs:
- section_grad: float32 [32, 256, 256], P('dom', 'tilt')
- scores: float32 [32], P('dom')
Inputs may be any that keep to these rules, and one draw needn't show every extreme that they name: `nbr_owner`: among the 32 neighbour entries of one spatial block's particles, at most 4 name the same owner block; some blocks reach 4.
All inputs are finite; a program needn't handle non-finite values.
Results may differ from a plain program's by a relative error of at most 0.013.
Values may be sent and summed in bfloat16 or wider, within the bound.
No kernel may reach another device: no remote copies, remote signals or barrier semaphores. Data moves between devices by JAX's collectives and lax.ppermute only.
A program may use at most 64 MiB of HBM per device.

v0:
```python
import jax
import jax.numpy as jnp
from jax import lax
from jax.sharding import PartitionSpec as P

OVL = 16


def split_dot(weights, bands):
    hi = weights.astype(jnp.bfloat16)
    rest = weights - hi.astype(jnp.float32)
    mid = rest.astype(jnp.bfloat16)
    low = (rest - mid.astype(jnp.float32)).astype(jnp.bfloat16)
    total = jnp.dot(hi, bands, preferred_element_type=jnp.float32)
    total = total + jnp.dot(mid, bands, preferred_element_type=jnp.float32)
    return total + jnp.dot(low, bands, preferred_element_type=jnp.float32)


def on_device(
    sections, images, slice_rows, slice_cols, ctf_filter, nbr_owner, nbr_local, nbr_side, nbr_weight
):
    own_count = sections.shape[0]
    pixels = sections.shape[1]
    tilt_count = images.shape[1]
    neighbours = nbr_local.shape[1]
    peer_count = lax.axis_size("dom")
    total = own_count * peer_count
    me = lax.axis_index("dom")
    band_size = tilt_count * OVL * pixels
    target = nbr_owner.reshape(own_count, neighbours) * own_count + nbr_local
    every = jnp.arange(total)
    hits = target[:, :, None] == every[None, None, :]
    fwd = [
        jnp.sum(jnp.where(hits & (nbr_side == s)[:, :, None], nbr_weight[:, :, None], 0.0), axis=1)
        for s in (0, 1)
    ]
    target_all = lax.all_gather(target, "dom", axis=0, tiled=True)
    side_all = lax.all_gather(nbr_side, "dom", axis=0, tiled=True)
    weight_all = lax.all_gather(nbr_weight, "dom", axis=0, tiled=True)
    halfway = jnp.einsum(
        "kij,tlj->ktil", sections, slice_cols, preferred_element_type=jnp.float32
    ).astype(jnp.bfloat16)
    projected = jnp.einsum(
        "tai,ktil->ktal", slice_rows, halfway, preferred_element_type=jnp.float32
    ).astype(jnp.bfloat16)
    edges = jnp.stack((projected[:, :, :OVL], projected[:, :, pixels - OVL :]), axis=1)
    edges_all = lax.all_gather(edges, "dom", axis=0, tiled=True)
    lower_part = split_dot(fwd[0], edges_all[:, 0].reshape(total, band_size))
    upper_part = split_dot(fwd[1], edges_all[:, 1].reshape(total, band_size))
    lower_part = lower_part.reshape(own_count, tilt_count, OVL, pixels)
    upper_part = upper_part.reshape(own_count, tilt_count, OVL, pixels)
    residual = images.astype(jnp.float32) - projected.astype(jnp.float32)
    residual = residual.at[:, :, :OVL].add(-upper_part)
    residual = residual.at[:, :, pixels - OVL :].add(-lower_part)
    residual_portion = residual.astype(jnp.bfloat16)
    smoothed_images = jnp.einsum(
        "tab,ktbc->ktac", ctf_filter, residual_portion, preferred_element_type=jnp.float32
    ).astype(jnp.bfloat16)
    filtered_images = jnp.einsum(
        "ktac,tdc->ktad", smoothed_images, ctf_filter, preferred_element_type=jnp.float32
    )
    score_part = jnp.sum(filtered_images * filtered_images, axis=(1, 2, 3))
    tilt_groups = lax.axis_size("tilt")
    scores = 0.5 * lax.psum(score_part, "tilt") / (tilt_count * tilt_groups * pixels * pixels)
    filtered_portion = filtered_images.astype(jnp.bfloat16)
    reverse_pass = jnp.einsum(
        "tab,ktac->ktbc", ctf_filter, filtered_portion, preferred_element_type=jnp.float32
    ).astype(jnp.bfloat16)
    weighted = jnp.einsum(
        "ktbc,tcd->ktbd", reverse_pass, ctf_filter, preferred_element_type=jnp.float32
    ).astype(jnp.bfloat16)
    grad_bands = jnp.stack((weighted[:, :, :OVL], weighted[:, :, pixels - OVL :]), axis=1)
    grad_all = lax.all_gather(grad_bands, "dom", axis=0, tiled=True)
    mine = me * own_count + jnp.arange(own_count)
    named = target_all[None, :, :] == mine[:, None, None]
    back = [
        jnp.sum(jnp.where(named & (side_all == s)[None], weight_all[None], 0.0), axis=2)
        for s in (0, 1)
    ]
    add_top = split_dot(back[0], grad_all[:, 1].reshape(total, band_size))
    add_bottom = split_dot(back[1], grad_all[:, 0].reshape(total, band_size))
    add_top = add_top.reshape(own_count, tilt_count, OVL, pixels)
    add_bottom = add_bottom.reshape(own_count, tilt_count, OVL, pixels)
    proj_grad = weighted.astype(jnp.float32)
    proj_grad = proj_grad.at[:, :, :OVL].add(add_top)
    proj_grad = proj_grad.at[:, :, pixels - OVL :].add(add_bottom)
    proj_half = proj_grad.astype(jnp.bfloat16)
    upward = jnp.einsum(
        "tai,ktal->ktil", slice_rows, proj_half, preferred_element_type=jnp.float32
    ).astype(jnp.bfloat16)
    partial_grad = -jnp.einsum(
        "ktil,tlj->kij", upward, slice_cols, preferred_element_type=jnp.float32
    )
    section_grad = lax.psum_scatter(partial_grad, "tilt", scatter_dimension=1, tiled=True)
    return (section_grad, scores)


def solution(mesh):
    in_specs = (
        P("dom", None, None),
        P("dom", "tilt", None, None),
        P("tilt", None, None),
        P("tilt", None, None),
        P("tilt", None, None),
        P("dom", None, None),
        P("dom", None),
        P("dom", None),
        P("dom", None),
    )
    out_specs = (P("dom", "tilt", None), P("dom"))
    return jax.shard_map(
        on_device, mesh=mesh, in_specs=in_specs, out_specs=out_specs, check_vma=False
    )
```

profile of v0, /device:TPU:0, one launch (start us, length us, event | category | flops | bytes accessed | tf_op | source)
XLA Modules:
  0.0 136.8 jit_solution(1483881849874437)
XLA Ops:
  7.2 0.0 copy-start
  7.2 0.0 all-gather.6.cloned.1.call-start
  7.2 1.9 %convert_subtract_fusion = (f32[2,2,256,256]{3,2,0,1:T(8,128)S(1)}, bf16[2,2,256,256]{3,2,0,1:T(8,128)(2,1)S(1)}) fusion(bf16[2,2,256,256]{3,2,1,0:T(8,128)(2,1)} %param.18, bf16[2,256,256]{2,1,0:T(8,128)(2,1)} %param.19, bf16[2,256,256]{2,1,0:T(8,128)(2,1)} %param.20, bf16[2,256,256]{2,1,0:T(8,128)(2,1)} %param.17), kind=kOutput, calls=%fused_computation.26 | convolution fusion | flops 269746176 | bytes 2883584 | tf_op jit(solution)/shard_map/tai,ktil->ktal/dot_general | solution.py:43
  9.1 0.6 pad_maximum_fusion
  9.7 0.0 copy-start.5
  9.7 0.0 all-gather.6.cloned.1.call-update
  9.8 0.0 all-gather.8.cloned.1.call-start
  9.8 0.6 copy-done.5
  10.4 0.0 copy-start.6
  10.4 0.1 mul.19
  10.5 0.6 copy-done.6
  11.1 0.0 copy-start.4
  11.1 0.7 copy-done.4
  11.8 0.0 copy-start.3
  11.8 0.7 copy-done.3
  12.5 0.1 select_reduce_fusion.2
  12.6 38.9 %all-gather.6.cloned.1.call-done = bf16[32,2,2,16,256]{4,3,0,2,1:T(8,128)(2,1)} async-done(((bf16[2,2,2,16,256]{4,3,0,2,1:T(8,128)(2,1)}), bf16[32,2,2,16,256]{4,3,0,2,1:T(8,128)(2,1)}) %all-gather.6.cloned.1.call-update) | async-done | bytes 1048592 | tf_op jit(solution)/shard_map/all_gather | solution.py:47
  51.5 1.3 fusion.53
  52.7 0.1 copy.39
  52.8 0.2 reshape_squeeze.12
  53.1 0.2 fusion.37
  53.2 0.2 convolution_add_fusion.7
  53.4 0.2 fusion.1
  53.6 0.1 copy.41
  53.7 0.2 reshape_squeeze.13
  54.0 0.2 fusion.41
  54.1 0.2 convolution_add_fusion.5
  54.3 0.2 fusion
  54.6 0.0 copy-done
  54.6 0.7 multiply_reduce_fusion
  55.3 0.6 fusion.58
  55.9 0.6 pad_maximum_fusion.1
  56.6 0.0 all-gather.8.cloned.1.call-update
  56.6 0.0 reduce-scatter.2.cloned.1.call-start
  56.7 19.3 %all-gather.2 = f32[16,2,16]{2,1,0:T(2,128)S(1)} all-gather(f32[1,2,16]{2,1,0:T(2,128)S(1)} %bitcast.146), channel_id=1, replica_groups=mesh['tilt'=2,'dom'=16] {'dom'}, dimensions={0}, use_global_device_ids=true | all-gather | bytes 2176 | tf_op jit(solution)/shard_map/all_gather | solution.py:39
  76.0 0.1 copy.49
  76.1 17.4 %all-gather = s32[16,2,16]{2,1,0:T(2,128)S(1)} all-gather(s32[1,2,16]{2,1,0:T(2,128)S(1)} %bitcast.145), channel_id=1, replica_groups=mesh['tilt'=2,'dom'=16] {'dom'}, dimensions={0}, use_global_device_ids=true | all-gather | bytes 2176 | tf_op jit(solution)/shard_map/all_gather | solution.py:37
  93.5 0.1 copy.47
  93.5 18.8 %all-gather.1 = s32[16,2,16]{2,1,0:T(2,128)S(1)} all-gather(s32[1,2,16]{2,1,0:T(2,128)S(1)} %bitcast.147), channel_id=1, replica_groups=mesh['tilt'=2,'dom'=16] {'dom'}, dimensions={0}, use_global_device_ids=true | all-gather | bytes 2176 | tf_op jit(solution)/shard_map/all_gather | solution.py:38
  112.4 0.1 copy.52
  112.5 0.1 copy.48
  112.6 0.1 select_reduce_fusion
  112.7 0.0 all-gather.8.cloned.1.call-done
  112.7 1.3 fusion.52
  114.0 0.1 copy.50
  114.0 0.2 reshape_squeeze.14
  114.3 0.2 fusion.45
  114.5 0.2 convolution_add_fusion.3
  114.7 0.2 convolution_add_fusion.2
  114.9 0.1 copy.53
  114.9 0.2 reshape_squeeze.15
  115.2 0.2 fusion.49
  115.4 0.2 convolution_add_fusion.1
  115.6 0.2 convolution_add_fusion
  115.8 0.0 copy-start.1
  115.8 0.0 copy-start.2
  115.9 0.9 copy-done.1
  116.7 0.1 copy-done.2
  116.8 1.5 %fusion.9 = f32[2,256,256]{2,1,0:T(8,128)} fusion(bf16[2,256,256]{2,1,0:T(8,128)(2,1)S(1)} %copy-done.1, bf16[2,256,256]{2,1,0:T(8,128)(2,1)S(1)} %copy-done.2, f32[2,2,256,256]{3,2,0,1:T(8,128)S(1)} %fusion.30), kind=kOutput, calls=%fused_computation.24 | convolution fusion | flops 269090816 | bytes 2097152 | tf_op jit(solution)/shard_map/ktil,tlj->kij/dot_general | solution.py:91
  118.3 0.0 reduce-scatter.2.cloned.1.call-update
  118.3 4.9 %psum.7 = f32[2]{0:T(128)S(1)} all-reduce(f32[2]{0:T(128)S(1)} %get-tuple-element.70), channel_id=1, replica_groups=mesh['tilt'=2,'dom'=16] {'tilt'}, use_global_device_ids=true, to_apply=%region_6.7 | all-reduce | flops 2 | bytes 16 | tf_op jit(solution)/shard_map/psum | solution.py:64
  123.3 0.5 broadcast_multiply_fusion.1
  123.8 6.5 %reduce-scatter.2.cloned.1.call-done = f32[2,128,256]{2,1,0:T(8,128)} async-done(((f32[2,256,256]{2,1,0:T(8,128)}), f32[2,128,256]{2,1,0:T(8,128)}) %reduce-scatter.2.cloned.1.call-update) | async-done | bytes 262160 | tf_op jit(solution)/shard_map/reduce_scatter | solution.py:94
  (17 shorter events, 0.2 us)
Async XLA Ops:
  7.2 47.4 %copy-start = (bf16[2,256,256]{2,1,0:T(8,128)(2,1)S(1)}, bf16[2,256,256]{2,1,0:T(8,128)(2,1)}, u32[]{:S(2)}) copy-start(bf16[2,256,256]{2,1,0:T(8,128)(2,1)} %param.21) | copy-start | bytes 786436
  7.2 44.3 %all-gather.6.cloned.1.call-start = ((), (), s32[]{:S(2)}) async-start(), calls=%async_computation.1 | async-start | bytes 1114112 | tf_op jit(solution)/shard_map/all_gather | solution.py:47
  9.7 0.7 copy-start.5
  9.8 102.9 %all-gather.8.cloned.1.call-start = ((), (), s32[]{:S(2)}) async-start(), calls=%async_computation.2 | async-start | bytes 1114112 | tf_op jit(solution)/shard_map/all_gather | solution.py:73
  10.4 0.7 copy-start.6
  11.1 0.7 copy-start.4
  11.8 0.7 copy-start.3
  56.6 73.7 %reduce-scatter.2.cloned.1.call-start = ((), (), s32[]{:S(2)}) async-start(), calls=%async_computation.3 | async-start | bytes 786432 | tf_op jit(solution)/shard_map/reduce_scatter | solution.py:94
  115.8 1.0 copy-start.1
  115.8 1.0 copy-start.2
Sparse Core Ops, SparseCore 0:
  10.8 40.6 all-gather.5
  56.7 36.8 all-gather.7
  118.5 11.8 reduce-scatter.1
where the time goes:
time: 137 us
  blocking collectives  60.5 us (44%)
  waiting for transfers between devices  45.5 us (33%)
  between operations  14 us (10%)
  local copies, waits for them, and re-layouts  7.73 us (6%)
  matrix products  6.92 us (5%)
  other arithmetic  2.08 us (2%)
    all_gather x1, waiting for transfers between devices, on_device(): edges_all = lax.all_gather(edges, 'dom', axis=0, tiled=True)  38.9 us
    all_gather x1, blocking collectives, on_device(): weight_all = lax.all_gather(nbr_weight, 'dom', axis=0, tiled=True)  19.3 us
    all_gather x1, blocking collectives, on_device(): side_all = lax.all_gather(nbr_side, 'dom', axis=0, tiled=True)  18.8 us
    all_gather x1, blocking collectives, on_device(): target_all = lax.all_gather(target, 'dom', axis=0, tiled=True)  17.4 us
    reduce_scatter x1, waiting for transfers between devices, on_device(): lax.psum_scatter(partial_grad, 'tilt', scatter_dimension=1, tiled=True)  6.51 us
    psum x1, blocking collectives, on_device(): lax.psum(score_part, 'tilt')  4.94 us
    unnamed x20, local copies, waits for them, and re-layouts  3.68 us
  transfers between devices with their start and end apart: 3, of which 2 were waited for; matrix products, arithmetic and copies ran while one was open for 1% of the time, Pallas kernels for 0%

commit v1 on v0

--- a/solution.py
+++ b/solution.py
@@ -4,6 +4,29 @@
 from jax.sharding import PartitionSpec as P
 
 OVL = 16
+
+
+def in_order(parts, dim):
+    shape = list(parts.shape[1:])
+    shape[dim] *= parts.shape[0]
+    return jnp.moveaxis(parts, 0, dim).reshape(shape)
+
+
+def grow_blocks(value, axis):
+    devices, position = (lax.axis_size(axis), lax.axis_index(axis))
+    pieces, bit = (value[None], 1)
+    while bit < devices:
+        partner_block = lax.ppermute(pieces, axis, [(i, i ^ bit) for i in range(devices)])
+        low = position & bit == 0
+        pieces = jnp.concatenate(
+            [jnp.where(low, pieces, partner_block), jnp.where(low, partner_block, pieces)]
+        )
+        bit *= 2
+    return pieces
+
+
+def doubled_up(array, axis, dim):
+    return in_order(grow_blocks(array, axis), dim)
 
 
 def split_dot(weights, bands):
@@ -36,7 +59,7 @@
     ]
     target_all = lax.all_gather(target, "dom", axis=0, tiled=True)
     side_all = lax.all_gather(nbr_side, "dom", axis=0, tiled=True)
-    weight_all = lax.all_gather(nbr_weight, "dom", axis=0, tiled=True)
+    weight_all = doubled_up(nbr_weight, "dom", 0)
     halfway = jnp.einsum(
         "kij,tlj->ktil", sections, slice_cols, preferred_element_type=jnp.float32
     ).astype(jnp.bfloat16)

time: 137 us -> 128 us (0.934)
  blocking collectives: 60.5 us -> 43.1 us
  waiting for transfers between devices: 45.5 us -> 52.6 us
    all_gather x1 -> x0, blocking collectives: 19.3 us -> none  [on_device(): weight_all = lax.all_gather(nbr_weight, 'dom', axis=0, tiled=True)]
    ppermute x0 -> x4, waiting for transfers between devices: none -> 7.11 us  [grow_blocks(): lax.ppermute(pieces, axis, [(i, i ^ bit) for i in range(devices)])]
    all_gather x1, blocking collectives: 17.4 us -> 18.9 us  [on_device(): target_all = lax.all_gather(target, 'dom', axis=0, tiled=True)]
    unnamed x20 -> x19, local copies, waits for them, and re-layouts: 3.68 us -> 3.61 us
  transfers between devices with their start and end apart: 3 -> 7, of which waited for: 2 -> 4; matrix products, arithmetic and copies ran while one was open for 1% -> 1% of each run, Pallas kernels for 0% -> 0%
where the time goes in v1:
time: 128 us; the launch traced here: 127 us
  waiting for transfers between devices  52.6 us (41%)
  blocking collectives  43.1 us (34%)
  between operations  14.1 us (11%)
  local copies, waits for them, and re-layouts  7.73 us (6%)
  matrix products  6.92 us (5%)
  other arithmetic  2.15 us (2%)
    all_gather x1, waiting for transfers between devices, on_device(): edges_all = lax.all_gather(edges, 'dom', axis=0, tiled=True)  38.9 us
    all_gather x1, blocking collectives, on_device(): side_all = lax.all_gather(nbr_side, 'dom', axis=0, tiled=True)  19.3 us
    all_gather x1, blocking collectives, on_device(): target_all = lax.all_gather(target, 'dom', axis=0, tiled=True)  18.9 us
    ppermute x4, waiting for transfers between devices, grow_blocks(): lax.ppermute(pieces, axis, [(i, i ^ bit) for i in range(devices)])  7.11 us
    reduce_scatter x1, waiting for transfers between devices, on_device(): lax.psum_scatter(partial_grad, 'tilt', scatter_dimension=1, tiled=True)  6.51 us
    psum x1, blocking collectives, on_device(): lax.psum(score_part, 'tilt')  4.94 us
    unnamed x19, local copies, waits for them, and re-layouts  3.61 us
  transfers between devices with their start and end apart: 7, of which 4 were waited for; matrix products, arithmetic and copies ran while one was open for 1% of the time, Pallas kernels for 0%

profile of v1, /device:TPU:0, one launch (start us, length us, event | category | flops | bytes accessed | tf_op | source)
XLA Modules:
  0.0 127.3 jit_solution(13239194027943825999)
XLA Ops:
  7.2 0.0 copy-start
  7.2 0.0 all-gather.5.cloned.1.call-start
  7.2 1.9 %convert_subtract_fusion = (f32[2,2,256,256]{3,2,0,1:T(8,128)S(1)}, bf16[2,2,256,256]{3,2,0,1:T(8,128)(2,1)S(1)}) fusion(bf16[2,2,256,256]{3,2,1,0:T(8,128)(2,1)} %param.18, bf16[2,256,256]{2,1,0:T(8,128)(2,1)} %param.19, bf16[2,256,256]{2,1,0:T(8,128)(2,1)} %param.20, bf16[2,256,256]{2,1,0:T(8,128)(2,1)} %param.17), kind=kOutput, calls=%fused_computation.26 | convolution fusion | flops 269746176 | bytes 2883584 | tf_op jit(solution)/shard_map/tai,ktil->ktal/dot_general | solution.py:66
  9.1 0.6 pad_maximum_fusion
  9.7 0.0 all-gather.5.cloned.1.call-update
  9.8 0.0 all-gather.7.cloned.1.call-start
  9.8 0.6 copy-done.5
  10.4 0.1 mul.19
  10.5 0.6 copy-done.6
  11.1 0.7 copy-done.3
  11.8 0.7 copy-done.4
  12.5 0.1 select_reduce_fusion.2
  12.6 38.9 %all-gather.5.cloned.1.call-done = bf16[32,2,2,16,256]{4,3,0,2,1:T(8,128)(2,1)} async-done(((bf16[2,2,2,16,256]{4,3,0,2,1:T(8,128)(2,1)}), bf16[32,2,2,16,256]{4,3,0,2,1:T(8,128)(2,1)}) %all-gather.5.cloned.1.call-update) | async-done | bytes 1048592 | tf_op jit(solution)/shard_map/all_gather | solution.py:70
  51.5 1.3 fusion.53
  52.7 0.1 copy.39
  52.8 0.2 reshape_squeeze.12
  53.1 0.2 fusion.37
  53.2 0.2 convolution_add_fusion.7
  53.4 0.2 fusion.1
  53.6 0.1 copy.41
  53.7 0.2 reshape_squeeze.13
  54.0 0.2 fusion.41
  54.1 0.2 convolution_add_fusion.5
  54.3 0.2 fusion
  54.6 0.7 multiply_reduce_fusion
  55.3 0.6 fusion.58
  55.9 0.6 pad_maximum_fusion.1
  56.6 0.0 all-gather.7.cloned.1.call-update
  56.6 0.0 reduce-scatter.2.cloned.1.call-start
  56.7 0.3 collective-permute-start
  57.0 19.3 %all-gather.1 = s32[16,2,16]{2,1,0:T(2,128)S(1)} all-gather(s32[1,2,16]{2,1,0:T(2,128)S(1)} %bitcast.148), channel_id=1, replica_groups=mesh['tilt'=2,'dom'=16] {'dom'}, dimensions={0}, use_global_device_ids=true | all-gather | bytes 2176 | tf_op jit(solution)/shard_map/all_gather | solution.py:61
  76.3 0.0 collective-permute-done
  76.3 0.1 collective-permute-start.1
  76.4 3.5 %collective-permute-done.1 = f32[2,2,16]{2,1,0:T(2,128)S(1)} collective-permute-done((f32[2,2,16]{2,1,0:T(2,128)S(1)}, f32[2,2,16]{2,1,0:T(2,128)S(1)}, u32[]{:S(2)}, u32[]{:S(2)}) %collective-permute-start.1) | collective-permute-done | bytes 288 | tf_op jit(solution)/shard_map/ppermute | solution.py:19
  80.0 0.1 collective-permute-start.2
  80.1 3.6 %collective-permute-done.2 = f32[4,2,16]{2,1,0:T(2,128)S(1)} collective-permute-done((f32[4,2,16]{2,1,0:T(2,128)S(1)}, f32[4,2,16]{2,1,0:T(2,128)S(1)}, u32[]{:S(2)}, u32[]{:S(2)}) %collective-permute-start.2) | collective-permute-done | bytes 544 | tf_op jit(solution)/shard_map/ppermute | solution.py:19
  83.7 0.1 collective-permute-start.3
  83.8 18.9 %all-gather = s32[16,2,16]{2,1,0:T(2,128)S(1)} all-gather(s32[1,2,16]{2,1,0:T(2,128)S(1)} %bitcast.147), channel_id=1, replica_groups=mesh['tilt'=2,'dom'=16] {'dom'}, dimensions={0}, use_global_device_ids=true | all-gather | bytes 2176 | tf_op jit(solution)/shard_map/all_gather | solution.py:60
  102.6 0.1 copy.47
  102.7 0.1 copy.52
  102.8 0.1 copy.48
  103.0 0.1 copy.49
  103.0 0.1 select_reduce_fusion
  103.1 0.0 all-gather.7.cloned.1.call-done
  103.2 1.3 fusion.52
  104.4 0.1 copy.50
  104.5 0.2 reshape_squeeze.14
  104.7 0.2 fusion.45
  104.9 0.2 convolution_add_fusion.3
  105.1 0.2 convolution_add_fusion.2
  105.3 0.1 copy.53
  105.4 0.2 reshape_squeeze.15
  105.6 0.2 fusion.49
  105.8 0.2 convolution_add_fusion.1
  106.0 0.2 convolution_add_fusion
  106.2 0.0 copy-start.1
  106.2 0.0 copy-start.2
  106.3 0.9 copy-done.1
  107.2 0.1 copy-done.2
  107.2 1.5 %fusion.9 = f32[2,256,256]{2,1,0:T(8,128)} fusion(bf16[2,256,256]{2,1,0:T(8,128)(2,1)S(1)} %copy-done.1, bf16[2,256,256]{2,1,0:T(8,128)(2,1)S(1)} %copy-done.2, f32[2,2,256,256]{3,2,0,1:T(8,128)S(1)} %fusion.30), kind=kOutput, calls=%fused_computation.24 | convolution fusion | flops 269090816 | bytes 2097152 | tf_op jit(solution)/shard_map/ktil,tlj->kij/dot_general | solution.py:114
  108.8 0.0 reduce-scatter.2.cloned.1.call-update
  108.8 4.9 %psum.7 = f32[2]{0:T(128)S(1)} all-reduce(f32[2]{0:T(128)S(1)} %get-tuple-element.78), channel_id=1, replica_groups=mesh['tilt'=2,'dom'=16] {'tilt'}, use_global_device_ids=true, to_apply=%region_6.7 | all-reduce | flops 2 | bytes 16 | tf_op jit(solution)/shard_map/psum | solution.py:87
  113.7 0.5 broadcast_multiply_fusion.1
  114.2 6.5 %reduce-scatter.2.cloned.1.call-done = f32[2,128,256]{2,1,0:T(8,128)} async-done(((f32[2,256,256]{2,1,0:T(8,128)}), f32[2,128,256]{2,1,0:T(8,128)}) %reduce-scatter.2.cloned.1.call-update) | async-done | bytes 262160 | tf_op jit(solution)/shard_map/reduce_scatter | solution.py:117
  (31 shorter events, 0.3 us)
Async XLA Ops:
  7.2 47.4 %copy-start = (bf16[2,256,256]{2,1,0:T(8,128)(2,1)S(1)}, bf16[2,256,256]{2,1,0:T(8,128)(2,1)}, u32[]{:S(2)}) copy-start(bf16[2,256,256]{2,1,0:T(8,128)(2,1)} %param.21) | copy-start | bytes 786436
  7.2 44.3 %all-gather.5.cloned.1.call-start = ((), (), s32[]{:S(2)}) async-start(), calls=%async_computation.1 | async-start | bytes 1114112 | tf_op jit(solution)/shard_map/all_gather | solution.py:70
  9.7 0.7 copy-start.5
  9.8 93.4 %all-gather.7.cloned.1.call-start = ((), (), s32[]{:S(2)}) async-start(), calls=%async_computation.2 | async-start | bytes 1114112 | tf_op jit(solution)/shard_map/all_gather | solution.py:96
  10.4 0.7 copy-start.6
  11.1 0.7 copy-start.3
  11.8 0.7 copy-start.4
  56.6 64.2 %reduce-scatter.2.cloned.1.call-start = ((), (), s32[]{:S(2)}) async-start(), calls=%async_computation.3 | async-start | bytes 786432 | tf_op jit(solution)/shard_map/reduce_scatter | solution.py:117
  56.7 19.6 %collective-permute-start = (f32[1,2,16]{2,1,0:T(2,128)S(1)}, f32[1,2,16]{2,1,0:T(2,128)S(1)}, u32[]{:S(2)}, u32[]{:S(2)}) collective-permute-start(f32[1,2,16]{2,1,0:T(2,128)S(1)} %bitcast.149), channel_id=1, source_target_pairs={{0,1},{1,0},{2,3},{3,2},{4,5},{5,4},{6,7},{7,6},{8,9},{9,8},{10,11... | collective-permute-start | bytes 392 | tf_op jit(solution)/shard_map/ppermute | solution.py:19
  76.3 3.6 %collective-permute-start.1 = (f32[2,2,16]{2,1,0:T(2,128)S(1)}, f32[2,2,16]{2,1,0:T(2,128)S(1)}, u32[]{:S(2)}, u32[]{:S(2)}) collective-permute-start(f32[2,2,16]{2,1,0:T(2,128)S(1)} %pad_maximum_fusion.5), channel_id=1, source_target_pairs={{0,2},{1,3},{2,0},{3,1},{4,6},{5,7},{6,4},{7,5},{8,10},{9,11},{10,... | collective-permute-start | bytes 776 | tf_op jit(solution)/shard_map/ppermute | solution.py:19
  80.0 3.7 %collective-permute-start.2 = (f32[4,2,16]{2,1,0:T(2,128)S(1)}, f32[4,2,16]{2,1,0:T(2,128)S(1)}, u32[]{:S(2)}, u32[]{:S(2)}) collective-permute-start(f32[4,2,16]{2,1,0:T(2,128)S(1)} %pad_maximum_fusion.4), channel_id=1, source_target_pairs={{0,4},{1,5},{2,6},{3,7},{4,0},{5,1},{6,2},{7,3},{8,12},{9,13},{10,... | collective-permute-start | bytes 1544 | tf_op jit(solution)/shard_map/ppermute | solution.py:19
  83.7 19.2 %collective-permute-start.3 = (f32[8,2,16]{2,1,0:T(2,128)S(1)}, f32[8,2,16]{2,1,0:T(2,128)S(1)}, u32[]{:S(2)}, u32[]{:S(2)}) collective-permute-start(f32[8,2,16]{2,1,0:T(2,128)S(1)} %pad_maximum_fusion.3), channel_id=1, source_target_pairs={{0,8},{1,9},{2,10},{3,11},{4,12},{5,13},{6,14},{7,15},{8,0},{9,1},... | collective-permute-start | bytes 3080 | tf_op jit(solution)/shard_map/ppermute | solution.py:19
  106.2 1.0 copy-start.1
  106.2 1.0 copy-start.2
Sparse Core Ops, SparseCore 0:
  10.8 40.6 all-gather.4
  56.7 36.8 all-gather.6
  108.9 11.8 reduce-scatter.1
